TPU v7x, 512 devices: a whole 4x4x16 slice. The times are simulated.
512 devices in a mesh: grp: 32 (over y, x, core), tp: 16 (over z).
Axes of the slice: x: 4, y: 4, z: 16, core: 2. Of those that a mesh axis runs over, the one named last changes fastest.
Arguments:
- trainer_increment: float32 [1024, 128, 128], P(('tp', 'grp')), may hold values from -0.3125 to 0.3125
- trainer_residual: float32 [1024, 128, 128], P(('tp', 'grp')), may hold values from -0.3125 to 0.3125
- partition_tile_indices: int32 [512, 2], P(('tp', 'grp')), may hold values from 0 to 1, as said below
- retained_tallies: int32 [512], P(('tp', 'grp')), may hold values from 0 to 2, as said below
- projection_parameters: bfloat16 [8192, 2048], P('tp'), may hold values from -0.0625 to 0.0625
- normalized_activations: bfloat16 [4, 32, 8192], P(None, 'grp', 'tp'), may hold values from -6 to 6
- rotated_questions: bfloat16 [4, 32, 8192], P(None, 'grp'), may hold values from -256 to 256
- stored_attention_memory: bfloat16 [32, 8192, 2048], P('grp', 'tp'), may hold values from -6 to 6
- memory_fill_lengths: int32 [32], P('grp'), may hold values from 2 to 8192, as said below
Outputs:
- new_error: float32 [1024, 128, 128], P(('tp', 'grp'))
- new_kv: bfloat16 [4, 32, 2048], P(None, 'grp', 'tp')
- attention: bfloat16 [4, 32, 8192], P(None, 'grp', 'tp')
Inputs may be any that keep to these rules, and one draw needn't show every extreme that they name: `partition_tile_indices`: each row lists the local block numbers of one shard, each once; only its first retained_tallies entries name surviving blocks. `retained_tallies`: some shard lists all 2 of its blocks in every draw. Row r's valid cache positions are 0 to memory_fill_lengths[r] - 1; some row has all 8192 in every draw.
All inputs are finite; a program needn't handle non-finite values.
Results may differ from a plain program's by a relative error of at most 0.02.
Values may be sent and summed in bfloat16 or wider, within the bound.
A program may use at most 64 MiB of HBM per device.

v0:
```python
import math
import jax
import jax.numpy as jnp
from jax import lax
from jax.sharding import PartitionSpec as P

HD = 128
BLK = 128
NEG = -1e30


def merged(array, axis, combine):
    everything = jax.tree.map(lambda part: lax.all_gather(part, axis), array)
    initial = jax.tree.map(lambda part: part[0], everything)

    def step(k, so_far):
        return combine(so_far, jax.tree.map(lambda part: part[k], everything))

    return lax.fori_loop(1, lax.axis_size(axis), step, initial)


def retained_tiles(partition_tile_indices, retained_tallies):
    slots = partition_tile_indices.shape[1]
    sorting_permutation = jnp.arange(slots, dtype=jnp.int32)
    enumerated_tiles = sorting_permutation[None, :] < retained_tallies[:, None]
    hits = (
        partition_tile_indices[:, :, None] == sorting_permutation[None, None, :]
    ) & enumerated_tiles[:, :, None]
    return jnp.any(hits, axis=1)


def combine(first, second):
    top_a, total_a, blended_first = first
    top_b, total_b, mixed_b = second
    top = jnp.maximum(top_a, top_b)
    scale_a = jnp.exp(top_a - top)
    scale_b = jnp.exp(top_b - top)
    total = total_a * scale_a + total_b * scale_b
    mixed = blended_first * scale_a[..., None] + mixed_b * scale_b[..., None]
    return (top, total, mixed)


def cache_partial(rotated_questions, stored_attention_memory, memory_fill_lengths, first):
    steps, rows, width = rotated_questions.shape
    span = stored_attention_memory.shape[1]
    heads_kv = stored_attention_memory.shape[2] // (2 * HD)
    group = width // HD // heads_kv
    scale = 1.0 / math.sqrt(HD)
    query = rotated_questions.reshape(steps, rows, heads_kv, group, HD)
    cache_rows_held = stored_attention_memory.reshape(rows, span, heads_kv, 2, HD)
    scores = (
        jnp.einsum(
            "srhgd,rphd->srhgp",
            query,
            cache_rows_held[:, :, :, 0],
            preferred_element_type=jnp.float32,
        )
        * scale
    )
    position = first + jnp.arange(span, dtype=jnp.int32)
    valid = (position[None, :] < memory_fill_lengths[:, None])[None, :, None, None, :]
    scores = jnp.where(valid, scores, NEG)
    top = jnp.max(scores, axis=-1)
    probs = jnp.where(valid, jnp.exp(scores - top[..., None]), 0.0)
    total = jnp.sum(probs, axis=-1)
    values = cache_rows_held[:, :, :, 1].astype(jnp.float32)
    mixed = jnp.einsum("srhgp,rphd->srhgd", probs, values, precision=lax.Precision.HIGHEST)
    heads = heads_kv * group
    return (
        top.reshape(steps, rows, heads),
        total.reshape(steps, rows, heads),
        mixed.reshape(steps, rows, heads, HD),
    )


def body(
    trainer_increment,
    trainer_residual,
    partition_tile_indices,
    retained_tallies,
    projection_parameters,
    normalized_activations,
    rotated_questions,
    stored_attention_memory,
    memory_fill_lengths,
):
    summed = trainer_increment + trainer_residual
    retain_markers = retained_tiles(partition_tile_indices, retained_tallies).reshape(-1)
    sent = jnp.where(
        retain_markers[:, None, None], summed.astype(jnp.bfloat16), jnp.zeros((), jnp.bfloat16)
    )
    new_error = summed - sent.astype(jnp.float32)
    blocks = lax.all_gather(sent, "grp", axis=0, tiled=True)
    local_feats, kvw = projection_parameters.shape
    update = (
        blocks.reshape(local_feats // BLK, kvw // BLK, BLK, BLK)
        .transpose(0, 2, 1, 3)
        .reshape(local_feats, kvw)
    )
    patched = (projection_parameters.astype(jnp.float32) + update.astype(jnp.float32)).astype(
        jnp.bfloat16
    )
    steps, local_rows, width = normalized_activations.shape
    partial_kv = jnp.dot(
        normalized_activations.reshape(steps * local_rows, width),
        patched,
        preferred_element_type=jnp.float32,
    )
    ranks = lax.axis_size("tp")
    rank = lax.axis_index("tp")
    columns = kvw // ranks
    kv_full = lax.psum(partial_kv, "tp").astype(jnp.bfloat16)
    kv_own = lax.dynamic_slice_in_dim(kv_full, rank * columns, columns, 1)
    new_kv = kv_own.reshape(steps, local_rows, columns)
    span = stored_attention_memory.shape[1]
    top, total, mixed = cache_partial(
        rotated_questions, stored_attention_memory, memory_fill_lengths, rank * span
    )
    heads = top.shape[2]
    own = heads // ranks
    top, total, mixed = merged((top, total, mixed), "tp", combine)
    top = lax.dynamic_slice_in_dim(top, rank * own, own, 2)
    total = lax.dynamic_slice_in_dim(total, rank * own, own, 2)
    mixed = lax.dynamic_slice_in_dim(mixed, rank * own, own, 2)
    heads_kv = kvw // (2 * HD)
    group = heads // heads_kv
    scale = 1.0 / math.sqrt(HD)
    fresh = kv_full.reshape(steps, local_rows, heads_kv, 2, HD)
    head_ids = (rank * own + jnp.arange(own, dtype=jnp.int32)) // group
    fresh = jnp.take(fresh, head_ids, axis=2)
    query = lax.dynamic_slice_in_dim(rotated_questions, rank * own * HD, own * HD, 2).reshape(
        steps, local_rows, own, HD
    )
    scores = (
        jnp.einsum("srjd,urjd->srju", query, fresh[:, :, :, 0], preferred_element_type=jnp.float32)
        * scale
    )
    step_ids = jnp.arange(steps, dtype=jnp.int32)
    causal = (step_ids[None, :] <= step_ids[:, None])[:, None, None, :]
    scores = jnp.where(causal, scores, NEG)
    peak = jnp.maximum(top, jnp.max(scores, axis=-1))
    probs = jnp.where(causal, jnp.exp(scores - peak[..., None]), 0.0)
    carried = jnp.exp(top - peak)
    denom = total * carried + jnp.sum(probs, axis=-1)
    values = fresh[:, :, :, 1].astype(jnp.float32)
    numer = mixed * carried[..., None] + jnp.einsum(
        "srju,urjd->srjd", probs, values, precision=lax.Precision.HIGHEST
    )
    attention = (numer / denom[..., None]).reshape(steps, local_rows, own * HD).astype(jnp.bfloat16)
    return (new_error, new_kv, attention)


def solution(mesh):
    placed = (
        P(("tp", "grp"), None, None),
        P(("tp", "grp"), None, None),
        P(("tp", "grp"), None),
        P(("tp", "grp")),
        P("tp", None),
        P(None, "grp", "tp"),
        P(None, "grp", None),
        P("grp", "tp", None),
        P("grp"),
    )
    return jax.shard_map(
        body,
        mesh=mesh,
        in_specs=placed,
        out_specs=(P(("tp", "grp"), None, None), P(None, "grp", "tp"), P(None, "grp", "tp")),
        check_vma=False,
    )
```

profile of v0, /device:TPU:2, one launch (start us, length us, event | category | flops | bytes accessed | tf_op | source)
XLA Modules:
  0.0 221.9 jit_solution(10214104289567611357)
XLA Ops:
  7.2 2.9 %copy.91 = bf16[1,512,2048]{1,2,0:T(8,128)(2,1)S(1)} copy(bf16[1,512,2048]{2,1,0:T(8,128)(2,1)} %param.18) | data formatting | bytes 4194304 | tf_op args[7]
  10.9 0.4 fusion.34
  11.2 1.1 convolution_bitcast_fusion.1
  12.4 0.7 copy.134
  13.8 0.1 and_reduce_fusion
  13.9 0.7 convert_select_fusion
  14.6 0.7 convert_subtract_fusion
  15.3 0.2 fusion.13
  15.6 0.1 all_gather_reshape.9
  15.7 35.6 %all_gather.13 = f32[16,4,1,64]{3,1,2,0:T(4,128)S(1)} all-gather(f32[1,4,1,64]{3,1,2,0:T(4,128)S(1)} %all_gather_reshape.9), channel_id=1, replica_groups=mesh['grp'=32,'tp'=16] {'tp'}, dimensions={0}, use_global_device_ids=true | all-gather | bytes 17408 | tf_op jit(solution)/shard_map/all_gather | solution.py:13
  51.3 0.1 all_gather_reshape.10
  51.4 26.1 %all_gather.14 = f32[16,4,1,64]{3,1,2,0:T(4,128)S(1)} all-gather(f32[1,4,1,64]{3,1,2,0:T(4,128)S(1)} %all_gather_reshape.10), channel_id=1, replica_groups=mesh['grp'=32,'tp'=16] {'tp'}, dimensions={0}, use_global_device_ids=true | all-gather | bytes 17408 | tf_op jit(solution)/shard_map/all_gather | solution.py:13
  77.5 13.1 %all-gather.5.cloned.1.call-done = f32[16,4,1,64,128]{4,3,2,1,0:T(8,128)} async-done(((f32[1,4,1,64,128]{4,3,2,1,0:T(8,128)}), f32[16,4,1,64,128]{4,3,2,1,0:T(8,128)}) %all-gather.5.cloned.1.call-update) | async-done | bytes 2097168 | tf_op jit(solution)/shard_map/all_gather | solution.py:13
  90.5 0.9 slice_bitcast_fusion.4
  91.5 17.1 %while.19 = (s32[]{:T(128)}, f32[4,1,64]{2,1,0:T(1,128)S(1)}, f32[4,1,64]{2,1,0:T(1,128)S(1)}, f32[4,1,64,128]{3,2,1,0:T(8,128)S(1)}, f32[16,4,1,64]{3,1,2,0:T(4...) while((s32[]{:T(128)}, f32[4,1,64]{2,1,0:T(1,128)S(1)}, ...), condition=%wide.region_5.6_spmd, body=%wide.region_4.5_spmd.sunk | while | flops 99845 | bytes 407703 | solution.py:19
  91.5 1.1 fusion.37
  92.7 1.1 fusion.37
  93.8 1.1 fusion.37
  94.9 1.1 fusion.37
  96.1 1.1 fusion.37
  97.2 1.1 fusion.37
  98.4 1.1 fusion.37
  99.5 1.1 fusion.37
  100.6 1.1 fusion.37
  101.8 1.1 fusion.37
  102.9 1.1 fusion.37
  104.1 1.1 fusion.37
  105.2 1.1 fusion.37
  106.3 1.1 fusion.37
  107.5 1.1 fusion.37
  108.6 0.1 copy.103
  108.7 40.8 %all-gather.3.cloned.1.call-done = bf16[64,128,128]{2,1,0:T(8,128)(2,1)} async-done(((bf16[2,128,128]{2,1,0:T(8,128)(2,1)}), bf16[64,128,128]{2,1,0:T(8,128)(2,1)}) %all-gather.3.cloned.1.call-update) | async-done | bytes 2097168 | tf_op jit(solution)/shard_map/all_gather | solution.py:93
  149.5 2.1 convert_bitcast_fusion
  151.6 2.4 %copy.90 = f32[4,128,16,128]{3,2,1,0:T(8,128)S(1)} copy(f32[4,128,16,128]{3,1,2,0:T(8,128)S(1)} %convert_bitcast_fusion) | data formatting | bytes 8388608 | tf_op jit(solution)/shard_map/convert_element_type | solution.py:100
  154.1 1.3 convolution_bitcast_fusion
  155.4 56.9 %psum.7 = bf16[4,2048]{1,0:T(4,128)(2,1)S(1)} all-reduce(f32[4,2048]{1,0:T(4,128)S(1)} %convolution_bitcast_fusion), channel_id=1, replica_groups=mesh['grp'=32,'tp'=16] {'tp'}, use_global_device_ids=true, to_apply=%region_1.2 | all-reduce | flops 8192 | bytes 49152 | tf_op jit(solution)/shard_map/psum | solution.py:112
  212.3 0.6 fusion.29
  212.8 0.6 gather_fusion
  213.4 0.1 bitcast_select_fusion
  213.5 0.1 fusion.35
  213.6 0.1 copy.107
  213.7 0.1 fusion.27
  213.8 0.1 copy.109
  213.9 0.1 copy.113
  214.0 0.1 fusion.31
  214.1 0.1 copy.114
  214.2 0.1 copy.108
  214.3 0.8 fusion.10
  (57 shorter events, 0.8 us)
Async XLA Ops:
  7.2 146.9 %copy-start = (bf16[4,1,512]{2,0,1:T(4,128)(2,1)S(1)}, bf16[4,1,512]{2,0,1:T(4,128)(2,1)}, u32[]{:S(2)}) copy-start(bf16[4,1,512]{2,0,1:T(4,128)(2,1)} %param.16) | copy-start | bytes 12292
  7.2 83.4 %all-gather.5.cloned.1.call-start = ((), (), s32[]{:S(2)}) async-start(), calls=%async_computation.1 | async-start | bytes 2228224 | tf_op jit(solution)/shard_map/all_gather | solution.py:13
  7.2 3.6 %copy-start.4 = (bf16[4,1,8192]{2,0,1:T(4,128)(2,1)S(1)}, bf16[4,1,8192]{2,0,1:T(4,128)(2,1)}, u32[]{:S(2)}) copy-start(bf16[4,1,8192]{2,0,1:T(4,128)(2,1)} %param.17) | copy-start | bytes 196612
  10.8 3.0 %copy-start.5 = (s32[1,2]{1,0:T(1,128)S(1)}, s32[1,2]{1,0:T(1,128)}, u32[]{:S(2)}) copy-start(s32[1,2]{1,0:T(1,128)} %param.13) | copy-start | bytes 28
  10.8 3.0 %copy-start.2 = (f32[2,128,128]{2,1,0:T(8,128)S(1)}, f32[2,128,128]{2,1,0:T(8,128)}, u32[]{:S(2)}) copy-start(f32[2,128,128]{2,1,0:T(8,128)} %param.11) | copy-start | bytes 393220
  10.8 3.0 %copy-start.3 = (f32[2,128,128]{2,1,0:T(8,128)S(1)}, f32[2,128,128]{2,1,0:T(8,128)}, u32[]{:S(2)}) copy-start(f32[2,128,128]{2,1,0:T(8,128)} %param.12) | copy-start | bytes 393220
  13.1 136.4 %all-gather.3.cloned.1.call-start = ((), (), s32[]{:S(2)}) async-start(), calls=%async_computation | async-start | bytes 2162688 | tf_op jit(solution)/shard_map/all_gather | solution.py:93
  151.6 2.5 %copy-start.1 = (bf16[512,2048]{1,0:T(8,128)(2,1)S(1)}, bf16[512,2048]{1,0:T(8,128)(2,1)}, u32[]{:S(2)}) copy-start(bf16[512,2048]{1,0:T(8,128)(2,1)} %param.15) | copy-start | bytes 6291460
Sparse Core Ops, SparseCore 0:
  13.2 77.3 all-gather.4
  93.7 55.7 all-gather.2
where the time goes:
time: 222 us
  blocking collectives  119 us (54%)
  waiting for transfers between devices  53.9 us (24%)
  other arithmetic  20.7 us (9%)
  between operations  15.5 us (7%)
  local copies, waits for them, and re-layouts  8.93 us (4%)
  matrix products  3.81 us (2%)
    all_gather x2, blocking collectives, merged(): everything = jax.tree.map(lambda part: lax.all_gather(part, axis), array)  61.6 us
    psum x1, blocking collectives, body(): kv_full = lax.psum(partial_kv, 'tp').astype(jnp.bfloat16)  56.9 us
    all_gather x1, waiting for transfers between devices, body(): blocks = lax.all_gather(sent, 'grp', axis=0, tiled=True)  40.8 us
    add x15, other arithmetic, combine(): mixed = blended_first * scale_a[..., None] + mixed_b * scale_b[..., None]  16.1 us
    all_gather x1, waiting for transfers between devices, merged(): everything = jax.tree.map(lambda part: lax.all_gather(part, axis), array)  13.1 us
  transfers between devices with their start and end apart: 2, of which 2 were waited for; matrix products, arithmetic and copies ran while one was open for 9% of the time, Pallas kernels for 0%

commit v1 on v0

--- a/solution.py
+++ b/solution.py
@@ -90,7 +90,9 @@
         retain_markers[:, None, None], summed.astype(jnp.bfloat16), jnp.zeros((), jnp.bfloat16)
     )
     new_error = summed - sent.astype(jnp.float32)
-    blocks = lax.all_gather(sent, "grp", axis=0, tiled=True)
+    blocks = jnp.concatenate(
+        lax.all_to_all(jnp.stack([sent] * lax.axis_size("grp")), "grp", 0, 0), axis=0
+    )
     local_feats, kvw = projection_parameters.shape
     update = (
         blocks.reshape(local_feats // BLK, kvw // BLK, BLK, BLK)

time: 222 us -> 174 us (0.78)
  waiting for transfers between devices: 53.9 us -> 0.02 us
  starting transfers between devices: 0.08 us -> 9.59 us
  blocking collectives: 119 us -> 114 us
    all_gather x1 -> x0, waiting for transfers between devices: 40.8 us -> none  [body(): blocks = lax.all_gather(sent, 'grp', axis=0, tiled=True)]
    all_gather x1, waiting for transfers between devices: 13.1 us -> 0.01 us  [merged(): everything = jax.tree.map(lambda part: lax.all_gather(part, axis), array)]
    all_to_all x0 -> x1, starting transfers between devices: none -> 9.55 us  [body(): lax.all_to_all(jnp.stack([sent] * lax.axis_size('grp')), 'grp', 0, 0)]
    psum x1, blocking collectives: 56.9 us -> 54.5 us  [body(): kv_full = lax.psum(partial_kv, 'tp').astype(jnp.bfloat16)]
  transfers between devices with their start and end apart: 2 -> 2, of which waited for: 2 -> 0; matrix products, arithmetic and copies ran while one was open for 9% -> 5% of each run, Pallas kernels for 0% -> 0%
where the time goes in v1:
time: 174 us; the launch traced here: 173 us
  blocking collectives  114 us (66%)
  other arithmetic  18.5 us (11%)
  between operations  15.5 us (9%)
  local copies, waits for them, and re-layouts  10.7 us (6%)
  starting transfers between devices  9.59 us (6%)
  matrix products  3.81 us (2%)
    all_gather x2, blocking collectives, merged(): everything = jax.tree.map(lambda part: lax.all_gather(part, axis), array)  59.8 us
    psum x1, blocking collectives, body(): kv_full = lax.psum(partial_kv, 'tp').astype(jnp.bfloat16)  54.5 us
    add x15, other arithmetic, combine(): mixed = blended_first * scale_a[..., None] + mixed_b * scale_b[..., None]  16.1 us
    all_to_all x1, starting transfers between devices, body(): lax.all_to_all(jnp.stack([sent] * lax.axis_size('grp')), 'grp', 0, 0)  9.55 us
  transfers between devices with their start and end apart: 2, of which 0 were waited for; matrix products, arithmetic and copies ran while one was open for 5% of the time, Pallas kernels for 0%

profile of v1, /device:TPU:2, one launch (start us, length us, event | category | flops | bytes accessed | tf_op | source)
XLA Modules:
  0.0 172.9 jit_solution(15371678002931211246)
XLA Ops:
  7.2 2.9 %copy.107 = bf16[1,512,2048]{1,2,0:T(8,128)(2,1)S(1)} copy(bf16[1,512,2048]{2,1,0:T(8,128)(2,1)} %param.18) | data formatting | bytes 4194304 | tf_op args[7]
  10.9 0.4 fusion.34
  11.2 1.2 convolution_bitcast_fusion.1
  12.4 0.7 copy.150
  13.7 0.1 and_reduce_fusion
  13.8 0.1 convert_select_fusion
  13.9 1.8 %stack.2 = bf16[32,2,128,128]{3,2,1,0:T(8,128)(2,1)} broadcast(bf16[2,128,128]{2,1,0:T(8,128)(2,1)S(1)} %convert_select_fusion), dimensions={1,2,3} | broadcast | bytes 2162688 | tf_op jit(solution)/shard_map/stack | solution.py:94
  15.7 9.5 %all-to-all-start = ((bf16[32,2,128,128]{3,2,1,0:T(8,128)(2,1)}), bf16[32,2,128,128]{3,2,1,0:T(8,128)(2,1)S(1)}, u32[]{:S(2)}, u32[]{:S(2)}) async-start(bf16[32,2,128,128]{3,2,1,0:T(8,128)(2,1)} %stack.2), calls=%async_computation | async-start | bytes 4194304 | tf_op jit(solution)/shard_map/all_to_all | solution.py:94
  25.3 0.1 all_gather_reshape.9
  25.4 33.6 %all_gather.9 = f32[16,4,1,64]{3,1,2,0:T(4,128)S(1)} all-gather(f32[1,4,1,64]{3,1,2,0:T(4,128)S(1)} %all_gather_reshape.9), channel_id=1, replica_groups=mesh['grp'=32,'tp'=16] {'tp'}, dimensions={0}, use_global_device_ids=true | all-gather | bytes 17408 | tf_op jit(solution)/shard_map/all_gather | solution.py:13
  59.0 0.2 fusion.13
  59.3 0.1 all_gather_reshape.10
  59.3 26.1 %all_gather.10 = f32[16,4,1,64]{3,1,2,0:T(4,128)S(1)} all-gather(f32[1,4,1,64]{3,1,2,0:T(4,128)S(1)} %all_gather_reshape.10), channel_id=1, replica_groups=mesh['grp'=32,'tp'=16] {'tp'}, dimensions={0}, use_global_device_ids=true | all-gather | bytes 17408 | tf_op jit(solution)/shard_map/all_gather | solution.py:13
  85.5 0.7 convert_subtract_fusion
  86.3 0.5 convert_bitcast_fusion
  86.8 2.4 %copy.106 = f32[4,128,16,128]{3,2,1,0:T(8,128)S(1)} copy(f32[4,128,16,128]{3,1,2,0:T(8,128)S(1)} %convert_bitcast_fusion) | data formatting | bytes 8388608 | tf_op jit(solution)/shard_map/convert_element_type | solution.py:102
  89.2 1.3 convolution_bitcast_fusion
  90.6 54.5 %psum.7 = bf16[4,2048]{1,0:T(4,128)(2,1)S(1)} all-reduce(f32[4,2048]{1,0:T(4,128)S(1)} %convolution_bitcast_fusion), channel_id=1, replica_groups=mesh['grp'=32,'tp'=16] {'tp'}, use_global_device_ids=true, to_apply=%region_1.2 | all-reduce | flops 8192 | bytes 49152 | tf_op jit(solution)/shard_map/psum | solution.py:114
  145.1 0.6 gather_fusion
  145.7 0.1 bitcast_select_fusion
  145.8 0.1 fusion.35
  145.9 0.1 copy.123
  146.0 0.6 fusion.29
  146.6 0.9 slice_bitcast_fusion.4
  147.5 17.1 %while.19 = (s32[]{:T(128)}, f32[4,1,64]{2,1,0:T(1,128)S(1)}, f32[4,1,64]{2,1,0:T(1,128)S(1)}, f32[4,1,64,128]{3,2,1,0:T(8,128)S(1)}, f32[16,4,1,64]{3,1,2,0:T(4...) while((s32[]{:T(128)}, f32[4,1,64]{2,1,0:T(1,128)S(1)}, ...), condition=%wide.region_5.6_spmd, body=%wide.region_4.5_spmd.sunk | while | flops 99845 | bytes 407703 | solution.py:19
  147.6 1.1 fusion.37
  148.7 1.1 fusion.37
  149.8 1.1 fusion.37
  151.0 1.1 fusion.37
  152.1 1.1 fusion.37
  153.3 1.1 fusion.37
  154.4 1.1 fusion.37
  155.5 1.1 fusion.37
  156.7 1.1 fusion.37
  157.8 1.1 fusion.37
  159.0 1.1 fusion.37
  160.1 1.1 fusion.37
  161.2 1.1 fusion.37
  162.4 1.1 fusion.37
  163.5 1.1 fusion.37
  164.6 0.1 copy.119
  164.7 0.1 fusion.27
  164.8 0.1 copy.125
  164.9 0.1 copy.129
  165.0 0.1 fusion.31
  165.1 0.1 copy.130
  165.2 0.1 copy.124
  165.3 0.8 fusion.10
  (57 shorter events, 0.7 us)
Async XLA Ops:
  7.2 82.1 %copy-start = (bf16[4,1,512]{2,0,1:T(4,128)(2,1)S(1)}, bf16[4,1,512]{2,0,1:T(4,128)(2,1)}, u32[]{:S(2)}) copy-start(bf16[4,1,512]{2,0,1:T(4,128)(2,1)} %param.16) | copy-start | bytes 12292
  7.2 139.4 %all-gather.2.cloned.1.call-start = ((), (), s32[]{:S(2)}) async-start(), calls=%async_computation.1 | async-start | bytes 2228224 | tf_op jit(solution)/shard_map/all_gather | solution.py:13
  7.2 3.6 %copy-start.4 = (bf16[4,1,8192]{2,0,1:T(4,128)(2,1)S(1)}, bf16[4,1,8192]{2,0,1:T(4,128)(2,1)}, u32[]{:S(2)}) copy-start(bf16[4,1,8192]{2,0,1:T(4,128)(2,1)} %param.17) | copy-start | bytes 196612
  10.8 2.9 %copy-start.5 = (s32[1,2]{1,0:T(1,128)S(1)}, s32[1,2]{1,0:T(1,128)}, u32[]{:S(2)}) copy-start(s32[1,2]{1,0:T(1,128)} %param.13) | copy-start | bytes 28
  10.8 3.0 %copy-start.2 = (f32[2,128,128]{2,1,0:T(8,128)S(1)}, f32[2,128,128]{2,1,0:T(8,128)}, u32[]{:S(2)}) copy-start(f32[2,128,128]{2,1,0:T(8,128)} %param.11) | copy-start | bytes 393220
  10.8 3.0 %copy-start.3 = (f32[2,128,128]{2,1,0:T(8,128)S(1)}, f32[2,128,128]{2,1,0:T(8,128)}, u32[]{:S(2)}) copy-start(f32[2,128,128]{2,1,0:T(8,128)} %param.12) | copy-start | bytes 393220
  15.7 70.5 %all-to-all-start = ((bf16[32,2,128,128]{3,2,1,0:T(8,128)(2,1)}), bf16[32,2,128,128]{3,2,1,0:T(8,128)(2,1)S(1)}, u32[]{:S(2)}, u32[]{:S(2)}) async-start(bf16[32,2,128,128]{3,2,1,0:T(8,128)(2,1)} %stack.2), calls=%async_computation | async-start | bytes 4194304 | tf_op jit(solution)/shard_map/all_to_all | solution.py:94
  86.8 2.5 %copy-start.1 = (bf16[512,2048]{1,0:T(8,128)(2,1)S(1)}, bf16[512,2048]{1,0:T(8,128)(2,1)}, u32[]{:S(2)}) copy-start(bf16[512,2048]{1,0:T(8,128)(2,1)} %param.15) | copy-start | bytes 6291460
Sparse Core Ops, SparseCore 0:
  13.2 77.2 all-gather.1
